TPU v7x, 32 devices: a whole 2x2x4 slice. The times are simulated.
32 devices in a mesh: tm: 8 (over z, y), grid: 4 (over x, core).
Axes of the slice: x: 2, y: 2, z: 4, core: 2. Of those that a mesh axis runs over, the one named last changes fastest.
Arguments:
- departure: float32 [16, 64, 3, 1024], P('tm', 'grid'), may hold values from -6 to 6
- obs_weight: float32 [16, 64], P('tm', 'grid'), may hold values from 0.2 to 2
- obs_block: int32 [16, 64], P('tm', 'grid'), may hold values from 0 to 7
- coarse_decay: float32 [3, 32, 1024], P(None, 'grid'), may hold values from 0.95 to 1
Outputs:
- adjoint: float32 [16, 3, 32, 1024], P('tm', None, 'grid')
- misfit: float32 [], replicated
- changes: float32 [3], replicated
Inputs may be any that keep to these rules, and one draw needn't show every extreme that they name: `obs_block`: several observations may name the same block.
All inputs are finite; a program needn't handle non-finite values.
Results may differ from a plain program's by a relative error of at most 0.0003.
Values sent between devices are 32-bit elements; how exact they have to be, the bound alone decides.
A program may use at most 64 MiB of HBM per device.

v0:
```python
import jax
import jax.numpy as jnp
from jax import lax
from jax.sharding import PartitionSpec as P

STEPS = 4
ITERS = 3
TILE_ROWS = 8
TILE_COLS = 128


wave_coef = 0.6
diffusion = 0.05
coriolis = 0.1
epsilon = 1e-06


def padded_2(value, sides, width):
    for axis, dim in sides:
        devices, length = (lax.axis_size(axis), value.shape[dim])
        up = [(i, (i + 1) % devices) for i in range(devices - 1)]
        down = [(j, i) for i, j in up]
        last = lax.slice_in_dim(value, length - width, length, axis=dim)
        first = lax.slice_in_dim(value, 0, width, axis=dim)
        before = lax.ppermute(last, axis, up)
        after = lax.ppermute(first, axis, down)
        value = jnp.concatenate([before, value, after], axis=dim)
    return value


def carried_in(value, axis, combine, identity):
    devices, here = (lax.axis_size(axis), lax.axis_index(axis))
    everything = jax.tree.map(lambda part: lax.all_gather(part, axis), value)
    start = jax.tree.map(
        lambda part, zero: jnp.broadcast_to(jnp.asarray(zero, part.dtype), part.shape),
        value,
        identity,
    )

    def hop(k, before):
        at = devices - 1 - k
        reached = at > here
        new = combine(before, jax.tree.map(lambda part: part[at], everything))
        return jax.tree.map(lambda a, b: jnp.where(reached, a, b), new, before)

    return lax.fori_loop(0, devices, hop, start)


def shifted(value, axis, by):
    devices = lax.axis_size(axis)
    pairs = [(i, i + by) for i in range(devices) if 0 <= i + by < devices]
    return lax.ppermute(value, axis, pairs)


def along_lon(values):
    return 0.5 * (jnp.roll(values, -1, -1) - jnp.roll(values, 1, -1))


def pad_rows(values):
    return jnp.pad(values, ((0, 0), (1, 1), (0, 0)))


def along_lat(values):
    padded = pad_rows(values)
    return 0.5 * (padded[:, 2:] - padded[:, :-2])


def laplace(values):
    padded = pad_rows(values)
    return (
        padded[:, 2:]
        + padded[:, :-2]
        + jnp.roll(values, -1, -1)
        + jnp.roll(values, 1, -1)
        - 4.0 * values
    )


def sweep_once(fields, inside):
    height, zonal, merid = (fields[:, 0], fields[:, 1], fields[:, 2])
    weight = inside[None, :, None]
    height_new = (
        height + wave_coef * (along_lon(zonal) + along_lat(merid)) + diffusion * laplace(height)
    ) * weight
    zonal_new = (
        zonal + wave_coef * along_lon(height_new) + coriolis * merid + diffusion * laplace(zonal)
    ) * weight
    merid_new = (
        merid + wave_coef * along_lat(height_new) - coriolis * zonal + diffusion * laplace(merid)
    ) * weight
    return jnp.stack([height_new, zonal_new, merid_new], axis=1)


def spread_tiles(scaled, blocks, row_count, lon_count):
    tile_rows_n = row_count // TILE_ROWS
    tile_cols_n = lon_count // TILE_COLS
    choose = (blocks[..., None] == jnp.arange(tile_rows_n * tile_cols_n, dtype=jnp.int32)).astype(
        jnp.float32
    )
    tiles = jnp.einsum("sob,soct->sbct", choose, scaled, precision=lax.Precision.HIGHEST)
    leading = scaled.shape[0]
    tiles = tiles.reshape(leading, tile_rows_n, tile_cols_n, 3, TILE_ROWS, TILE_COLS).transpose(
        0, 3, 1, 4, 2, 5
    )
    return tiles.reshape(leading, 3, row_count, lon_count)


def inside_rows(row_count, margin):
    band_index = lax.axis_index("grid")
    band_count = lax.axis_size("grid")
    global_row = band_index * row_count - margin + jnp.arange(row_count + 2 * margin)
    return ((global_row >= 0) & (global_row < row_count * band_count)).astype(jnp.float32)


def propagate(fields):
    row_count = fields.shape[2]
    margin = 2 * STEPS
    extended = padded_2(fields, (("grid", 2),), margin)
    inside = inside_rows(row_count, margin)
    for repeat in range(STEPS):
        extended = sweep_once(extended, inside)[:, :, 2:-2]
        inside = inside[2:-2]
    return extended


def run_chain(correction, coarse_decay, start):
    values = []
    current = start
    for offset in reversed(range(correction.shape[0])):
        current = coarse_decay * current + correction[offset]
        values.append(current)
    return jnp.stack(values[::-1], axis=0)


def compose_pair(earlier, later):
    return (later[0] * earlier[0], later[0] * earlier[1] + later[1])


def per_device(departure, obs_weight, obs_block, coarse_decay):
    sub_count = departure.shape[0]
    row_count = coarse_decay.shape[1]
    lon_count = coarse_decay.shape[2]
    window_total = lax.axis_size("tm") * sub_count
    window_first = lax.axis_index("tm") * sub_count
    position = (window_first + jnp.arange(sub_count)).astype(jnp.float32)
    emphasis = 1.0 + 2.0 * position / (window_total - 1)
    local_misfit = 0.5 * jnp.sum(
        emphasis[:, None] * obs_weight * jnp.sum(departure * departure, axis=(2, 3))
    )
    scaled = departure * (emphasis[:, None] * obs_weight)[:, :, None, None]
    forcing = spread_tiles(scaled, obs_block, row_count, lon_count)
    factor_here = coarse_decay**sub_count
    zeros_field = jnp.zeros_like(coarse_decay)

    def backward(correction):
        offset_here = run_chain(correction, coarse_decay, zeros_field)[0]
        composed = carried_in(
            (factor_here, offset_here),
            "tm",
            compose_pair,
            (jnp.ones_like(factor_here), zeros_field),
        )
        start = composed[1]
        return run_chain(correction, coarse_decay, start)

    misfit = lax.psum(local_misfit, ("tm", "grid"))
    adjoint = backward(forcing)
    changes = []
    for iteration in range(ITERS):
        following = shifted(adjoint[:1], "tm", -1)
        above = jnp.concatenate([adjoint[1:], following], axis=0)
        correction = propagate(above) - coarse_decay * above + forcing
        renewed = backward(correction)
        weights = emphasis[:, None, None, None]
        local_change = jnp.sum(weights * (renewed - adjoint) ** 2)
        local_size = jnp.sum(weights * renewed**2)
        total_change, total_size = lax.psum((local_change, local_size), ("tm", "grid"))
        changes.append(total_change / (total_size + epsilon))
        adjoint = renewed
    change_totals = jnp.stack(changes)
    return (adjoint, misfit, change_totals)


def solution(mesh):
    in_specs = (
        P("tm", "grid", None, None),
        P("tm", "grid"),
        P("tm", "grid"),
        P(None, "grid", None),
    )
    out_specs = (P("tm", None, "grid", None), P(), P())
    return jax.shard_map(
        per_device, mesh=mesh, in_specs=in_specs, out_specs=out_specs, check_vma=False
    )
```

profile of v0, /device:TPU:0, one launch (start us, length us, event | category | flops | bytes accessed | tf_op | source)
XLA Modules:
  0.0 274.9 jit_solution(18299048964590528448)
XLA Ops:
  0.7 1.2 multiply_reduce_fusion
  1.8 0.7 multiply_reduce_fusion.6
  2.5 0.7 copy-done.2
  3.2 0.3 convolution_bitcast_fusion
  3.6 0.9 copy-done
  4.5 33.9 %all-gather = f32[24,8,1024]{2,1,0:T(8,128)S(1)} all-gather(f32[3,8,1024]{2,1,0:T(8,128)S(1)} %get-tuple-element.777), channel_id=2, replica_groups=mesh['tm'=8,'grid'=4] {'tm'}, dimensions={0}, use_global_device_ids=true | all-gather | bytes 884736 | tf_op jit(solution)/shard_map/all_gather | solution.py:33
  38.4 32.1 %all-gather.1 = f32[24,8,1024]{2,1,0:T(8,128)S(1)} all-gather(f32[3,8,1024]{2,1,0:T(8,128)S(1)} %get-tuple-element.776), channel_id=3, replica_groups=mesh['tm'=8,'grid'=4] {'tm'}, dimensions={0}, use_global_device_ids=true | all-gather | bytes 884736 | tf_op jit(solution)/shard_map/all_gather | solution.py:33
  70.5 0.5 while.64
  71.0 1.3 collective-permute-start
  72.3 5.2 %collective-permute-done = f32[1,3,8,1024]{3,2,1,0:T(8,128)S(1)} collective-permute-done((f32[1,3,8,1024]{3,2,1,0:T(8,128)S(1)}, f32[1,3,8,1024]{3,2,1,0:T(8,128)S(1)}, u32[]{:S(2)}, u32[]{:S(2)}) %collective-permute-start) | collective-permute-done | bytes 98336 | tf_op jit(solution)/shard_map/ppermute | solution.py:52
  77.6 1.3 collective-permute-start.1
  78.9 1.3 collective-permute-start.2
  80.5 3.5 %collective-permute-done.2 = f32[2,3,8,1024]{3,2,1,0:T(8,128)S(1)} collective-permute-done((f32[2,3,8,1024]{3,2,1,0:T(8,128)S(1)}, f32[2,3,8,1024]{3,2,1,0:T(8,128)S(1)}, u32[]{:S(2)}, u32[]{:S(2)}) %collective-permute-start.2) | collective-permute-done | bytes 196640 | tf_op jit(solution)/shard_map/ppermute | solution.py:26
  89.3 32.0 %all-gather.2 = f32[24,8,1024]{2,1,0:T(8,128)S(1)} all-gather(f32[3,8,1024]{2,1,0:T(8,128)S(1)} %multiply_add_fusion.5), channel_id=4, replica_groups=mesh['tm'=8,'grid'=4] {'tm'}, dimensions={0}, use_global_device_ids=true | all-gather | bytes 884736 | tf_op jit(solution)/shard_map/all_gather | solution.py:33
  121.3 0.5 while.65
  121.8 1.3 collective-permute-start.3
  123.1 5.2 %collective-permute-done.3 = f32[1,3,8,1024]{3,2,1,0:T(8,128)S(1)} collective-permute-done((f32[1,3,8,1024]{3,2,1,0:T(8,128)S(1)}, f32[1,3,8,1024]{3,2,1,0:T(8,128)S(1)}, u32[]{:S(2)}, u32[]{:S(2)}) %collective-permute-start.3) | collective-permute-done | bytes 98336 | tf_op jit(solution)/shard_map/ppermute | solution.py:52
  128.4 1.3 collective-permute-start.4
  129.7 1.3 collective-permute-start.5
  131.0 6.2 %collective-permute-done.5 = f32[2,3,8,1024]{3,2,0,1:T(8,128)S(1)} collective-permute-done((f32[2,3,8,1024]{3,2,0,1:T(8,128)S(1)}, f32[2,3,8,1024]{3,2,0,1:T(8,128)S(1)}, u32[]{:S(2)}, u32[]{:S(2)}) %collective-permute-start.5) | collective-permute-done | bytes 196640 | tf_op jit(solution)/shard_map/ppermute | solution.py:26
  142.7 32.2 %all-gather.3 = f32[24,8,1024]{2,1,0:T(8,128)S(1)} all-gather(f32[3,8,1024]{2,1,0:T(8,128)S(1)} %multiply_add_fusion.3), channel_id=5, replica_groups=mesh['tm'=8,'grid'=4] {'tm'}, dimensions={0}, use_global_device_ids=true | all-gather | bytes 884736 | tf_op jit(solution)/shard_map/all_gather | solution.py:33
  174.9 0.5 while.66
  175.4 1.3 collective-permute-start.6
  176.7 5.2 %collective-permute-done.6 = f32[1,3,8,1024]{3,2,1,0:T(8,128)S(1)} collective-permute-done((f32[1,3,8,1024]{3,2,1,0:T(8,128)S(1)}, f32[1,3,8,1024]{3,2,1,0:T(8,128)S(1)}, u32[]{:S(2)}, u32[]{:S(2)}) %collective-permute-start.6) | collective-permute-done | bytes 98336 | tf_op jit(solution)/shard_map/ppermute | solution.py:52
  182.0 1.3 collective-permute-start.7
  184.0 1.5 collective-permute-start.8
  185.5 6.0 %collective-permute-done.8 = f32[2,3,8,1024]{3,2,0,1:T(8,128)S(1)} collective-permute-done((f32[2,3,8,1024]{3,2,0,1:T(8,128)S(1)}, f32[2,3,8,1024]{3,2,0,1:T(8,128)S(1)}, u32[]{:S(2)}, u32[]{:S(2)}) %collective-permute-start.8) | collective-permute-done | bytes 196640 | tf_op jit(solution)/shard_map/ppermute | solution.py:26
  197.0 32.5 %all-gather.4 = f32[24,8,1024]{2,1,0:T(8,128)S(1)} all-gather(f32[3,8,1024]{2,1,0:T(8,128)S(1)} %multiply_add_fusion.1), channel_id=6, replica_groups=mesh['tm'=8,'grid'=4] {'tm'}, dimensions={0}, use_global_device_ids=true | all-gather | bytes 884736 | tf_op jit(solution)/shard_map/all_gather | solution.py:33
  229.5 0.5 while.67
  230.0 1.4 multiply_reduce_fusion.5
  231.5 39.0 %all-reduce.48 = (f32[]{:T(128)}, f32[]{:T(128)}, f32[]{:T(128)}, f32[]{:T(128)}, f32[]{:T(128)}, /*index=5*/f32[]{:T(128)}, f32[]{:T(128)}) all-reduce(f32[]{:T(128)S(6)} %mul.1093, f32[]{:T(128)} %get-tuple-element.610, f32[]{:T(128)} %get-tuple-element.611, ...), channel_id=1, replica_groups=mesh['tm'=8,'grid'=4] {'tm','grid'}, use_global_device_ids=true, to_apply=%region_10.11 | all-reduce | flops 7 | bytes 56 | tf_op jit(solution)/shard_map/psum | solution.py:166
  274.4 0.6 pad_maximum_fusion.37
  (237 shorter events, 17.1 us)
Async XLA Ops:
  0.6 1.9 copy-start.1
  0.7 1.2 copy-start.3
  2.5 0.7 copy-start.2
  3.6 0.9 copy-start
  71.0 6.5 %collective-permute-start = (f32[1,3,8,1024]{3,2,1,0:T(8,128)S(1)}, f32[1,3,8,1024]{3,2,1,0:T(8,128)S(1)}, u32[]{:S(2)}, u32[]{:S(2)}) collective-permute-start(f32[1,3,8,1024]{3,2,1,0:T(8,128)S(1)} %get-tuple-element.679), channel_id=1, source_target_pairs={{4,0},{8,4},{12,8},{16,12},{20,16},{24,20},{28,24},{5,1},{9,5},{13... | collective-permute-start | bytes 294920 | tf_op jit(solution)/shard_map/ppermute | solution.py:52
  77.6 2.9 %collective-permute-start.1 = (f32[2,3,8,1024]{3,2,1,0:T(8,128)S(1)}, f32[2,3,8,1024]{3,2,1,0:T(8,128)S(1)}, u32[]{:S(2)}, u32[]{:S(2)}) collective-permute-start(f32[2,3,8,1024]{3,2,1,0:T(8,128)S(1)} %pad_maximum_fusion.7), channel_id=1, source_target_pairs={{0,1},{1,2},{2,3},{4,5},{5,6},{6,7},{8,9},{9,10},{10,11},{12,13},{... | collective-permute-start | bytes 589832 | tf_op jit(solution)/shard_map/ppermute | solution.py:25
  78.9 5.1 %collective-permute-start.2 = (f32[2,3,8,1024]{3,2,1,0:T(8,128)S(1)}, f32[2,3,8,1024]{3,2,1,0:T(8,128)S(1)}, u32[]{:S(2)}, u32[]{:S(2)}) collective-permute-start(f32[2,3,8,1024]{3,2,1,0:T(8,128)S(1)} %pad_maximum_fusion.7), channel_id=1, source_target_pairs={{1,0},{2,1},{3,2},{5,4},{6,5},{7,6},{9,8},{10,9},{11,10},{13,12},{... | collective-permute-start | bytes 589832 | tf_op jit(solution)/shard_map/ppermute | solution.py:26
  121.8 6.5 %collective-permute-start.3 = (f32[1,3,8,1024]{3,2,1,0:T(8,128)S(1)}, f32[1,3,8,1024]{3,2,1,0:T(8,128)S(1)}, u32[]{:S(2)}, u32[]{:S(2)}) collective-permute-start(f32[1,3,8,1024]{3,2,1,0:T(8,128)S(1)} %get-tuple-element.676), channel_id=1, source_target_pairs={{4,0},{8,4},{12,8},{16,12},{20,16},{24,20},{28,24},{5,1},{9,5},{13... | collective-permute-start | bytes 294920 | tf_op jit(solution)/shard_map/ppermute | solution.py:52
  128.4 2.6 collective-permute-start.4
  129.7 7.6 %collective-permute-start.5 = (f32[2,3,8,1024]{3,2,0,1:T(8,128)S(1)}, f32[2,3,8,1024]{3,2,0,1:T(8,128)S(1)}, u32[]{:S(2)}, u32[]{:S(2)}) collective-permute-start(f32[2,3,8,1024]{3,2,0,1:T(8,128)S(1)} %copy.23), channel_id=1, source_target_pairs={{1,0},{2,1},{3,2},{5,4},{6,5},{7,6},{9,8},{10,9},{11,10},{13,12},{... | collective-permute-start | bytes 589832 | tf_op jit(solution)/shard_map/ppermute | solution.py:26
  175.4 6.5 %collective-permute-start.6 = (f32[1,3,8,1024]{3,2,1,0:T(8,128)S(1)}, f32[1,3,8,1024]{3,2,1,0:T(8,128)S(1)}, u32[]{:S(2)}, u32[]{:S(2)}) collective-permute-start(f32[1,3,8,1024]{3,2,1,0:T(8,128)S(1)} %get-tuple-element.674), channel_id=1, source_target_pairs={{4,0},{8,4},{12,8},{16,12},{20,16},{24,20},{28,24},{5,1},{9,5},{13... | collective-permute-start | bytes 294920 | tf_op jit(solution)/shard_map/ppermute | solution.py:52
  182.0 3.4 %collective-permute-start.7 = (f32[2,3,8,1024]{3,2,0,1:T(8,128)S(1)}, f32[2,3,8,1024]{3,2,0,1:T(8,128)S(1)}, u32[]{:S(2)}, u32[]{:S(2)}) collective-permute-start(f32[2,3,8,1024]{3,2,0,1:T(8,128)S(1)} %copy.27), channel_id=1, source_target_pairs={{0,1},{1,2},{2,3},{4,5},{5,6},{6,7},{8,9},{9,10},{10,11},{12,13},{... | collective-permute-start | bytes 589832 | tf_op jit(solution)/shard_map/ppermute | solution.py:25
  184.0 7.6 %collective-permute-start.8 = (f32[2,3,8,1024]{3,2,0,1:T(8,128)S(1)}, f32[2,3,8,1024]{3,2,0,1:T(8,128)S(1)}, u32[]{:S(2)}, u32[]{:S(2)}) collective-permute-start(f32[2,3,8,1024]{3,2,0,1:T(8,128)S(1)} %copy.27), channel_id=1, source_target_pairs={{1,0},{2,1},{3,2},{5,4},{6,5},{7,6},{9,8},{10,9},{11,10},{13,12},{... | collective-permute-start | bytes 589832 | tf_op jit(solution)/shard_map/ppermute | solution.py:26
where the time goes:
time: 277 us; the launch traced here: 275 us
  blocking collectives  202 us (73%)
  waiting for transfers between devices  31.3 us (11%)
  starting transfers between devices  11.8 us (4%)
  other arithmetic  11.7 us (4%)
  local copies, waits for them, and re-layouts  10.8 us (4%)
  between operations  6.44 us (2%)
    all_gather x5, blocking collectives, carried_in(): everything = jax.tree.map(lambda part: lax.all_gather(part, axis), value)  163 us
    psum x1, blocking collectives, per_device(): misfit = lax.psum(local_misfit, ('tm', 'grid'))  39 us
    ppermute x3, waiting for transfers between devices, padded_2(): after = lax.ppermute(first, axis, down)  15.7 us
    ppermute x3, waiting for transfers between devices, shifted(): return lax.ppermute(value, axis, pairs)  15.6 us
  transfers between devices with their start and end apart: 9, of which 6 were waited for; matrix products, arithmetic and copies ran while one was open for 0% of the time, Pallas kernels for 0%

commit v1 on v0

v1 whole, which is shorter than its diff:
```python
import functools

import jax
import jax.numpy as jnp
from jax import lax
from jax.experimental import pallas as pl
from jax.experimental.pallas import tpu as pltpu
from jax.sharding import PartitionSpec as P

STEPS = 4
ITERS = 3
TILE_ROWS = 8
LANES = 128
CORES = 2
PAD = 32

wave_coef = 0.6
diffusion = 0.05
coriolis = 0.1
epsilon = 1e-06

MESH = pl.DeviceIdType.MESH
f32 = jnp.float32


def fine(p, q, r, row):
    rows = p.shape[0]

    def west_east(v):
        return pltpu.roll(v, 1, 1), pltpu.roll(v, LANES - 1, 1)

    def up_down(v):
        above = jnp.where(row == 0, 0.0, pltpu.roll(v, 1, 0))
        below = jnp.where(row == rows - 1, 0.0, pltpu.roll(v, rows - 1, 0))
        return above, below

    half = 0.5 * wave_coef
    keep = 1.0 - 4.0 * diffusion
    for _ in range(STEPS):
        pw, pe = west_east(p)
        pu, pd = up_down(p)
        qw, qe = west_east(q)
        qu, qd = up_down(q)
        rw, re = west_east(r)
        ru, rd = up_down(r)
        p = keep * p + half * ((qe - qw) + (rd - ru)) + diffusion * ((pw + pe) + (pu + pd))
        nw, ne = west_east(p)
        nu, nd = up_down(p)
        q, r = (
            keep * q + half * (ne - nw) + coriolis * r + diffusion * ((qw + qe) + (qu + qd)),
            keep * r + half * (nd - nu) - coriolis * q + diffusion * ((rw + re) + (ru + rd)),
        )
    return p, q, r


def kernel(T, G, dep, wt, blk, dec, adj, chg, mis, *scratch):
    (forc, win, recv, dwin, drecv, state, hold, delta, pack, ret, srow, sret, misv, misr) = scratch[:14]
    (snd, rcv, fsnd, frcv, dsnd, drcv, dfsnd, dfrcv, rsnd, rrcv, ssnd, srcv, msem) = scratch[14:]
    SD, OD, NF, TILE = dep.shape
    NLON = dec.shape[2]
    NB = NLON // LANES
    X = G // CORES
    NC = T * X
    S = NLON // NC
    R = LANES // S
    K = T * SD
    NI = SD * NF
    NV = pack.shape[1]
    rows = G * TILE_ROWS
    t = lax.axis_index("tm")
    g = lax.axis_index("grid")
    core = lax.rem(g, CORES)
    x = lax.div(g, CORES)
    c = t * X + x
    sibling = {"tm": t, "grid": x * CORES + (1 - core)}

    def peer(chip):
        return {"tm": lax.div(chip, X), "grid": lax.rem(chip, X) * CORES + core}

    def slot(chip):
        return lax.div(chip, X), lax.rem(chip, X) * CORES + core

    barrier = pltpu.get_barrier_semaphore()

    def greet(j, carry):
        pl.semaphore_signal(barrier, inc=1, device_id=peer(lax.rem(c + j, NC)), device_id_type=MESH)
        return carry

    lax.fori_loop(1, NC, greet, 0)
    pl.semaphore_signal(barrier, inc=1, device_id=sibling, device_id_type=MESH)

    sub = lax.broadcasted_iota(jnp.int32, (TILE_ROWS, LANES), 0)
    lane = lax.broadcasted_iota(jnp.int32, (TILE_ROWS, LANES), 1)
    cost = jnp.zeros((NF, NLON), f32)
    for s in range(SD):
        emph = 1.0 + 2.0 * (t * SD + s).astype(f32) / (K - 1)
        tiles = [[jnp.zeros((TILE_ROWS, LANES), f32) for _ in range(NB)] for _ in range(NF)]
        for o in range(OD):
            weight = emph * wt[s, o]
            choose = jnp.where(sub == blk[s, o], weight, 0.0)
            block = dep[s, o]
            cost = cost + (weight * block) * block
            for f in range(NF):
                for r in range(NB):
                    piece = dep[s, o, pl.ds(f, 1), pl.ds(r * LANES, LANES)]
                    tiles[f][r] = tiles[f][r] + choose * piece
        for f in range(NF):
            for r in range(NB):
                forc[pl.ds((s * NF + f) * NB * TILE_ROWS + r, NB, TILE_ROWS), :] = tiles[f][r]
    cost_row = jnp.sum(cost, axis=0, keepdims=True)
    total = cost_row[:, :LANES]
    for r in range(1, NB):
        total = total + cost_row[:, r * LANES : (r + 1) * LANES]
    misv[...] = total

    def window(read, chip):
        start = lax.rem(chip * S - PAD + NLON, NLON)
        b0 = lax.div(start, LANES)
        off = lax.rem(start, LANES)
        b1 = lax.rem(b0 + 1, NB)
        both = jnp.where(lane >= off, read(b0), read(b1))
        return pltpu.roll(both, lax.rem(LANES - off, LANES), 1)

    def cut(chip, carry):
        for i in range(NI):
            def read(b, i=i):
                at = pl.multiple_of((i * NB + b) * TILE_ROWS, TILE_ROWS)
                return forc[pl.ds(at, TILE_ROWS), :]
            win[chip, i] = window(read, chip)
        return carry

    lax.fori_loop(0, NC, cut, 0)
    for xx in range(X):
        for f in range(NF):
            def read(b, f=f):
                return dec[f, :, pl.ds(pl.multiple_of(b * LANES, LANES), LANES)]
            dwin[xx, f] = window(read, t * X + xx)

    pl.semaphore_wait(barrier, NC)

    def scatter(chip):
        return pltpu.make_async_remote_copy(
            src_ref=win.at[chip], dst_ref=recv.at[t, g], send_sem=snd.at[chip], recv_sem=rcv.at[c],
            device_id=peer(chip), device_id_type=MESH)

    def arrival(chip):
        tt, gg = slot(chip)
        return pltpu.make_async_remote_copy(
            src_ref=win.at[chip], dst_ref=recv.at[tt, gg], send_sem=snd.at[chip], recv_sem=rcv.at[chip],
            device_id=peer(chip), device_id_type=MESH)

    def forward(chip):
        tt, gg = slot(chip)
        return pltpu.make_async_remote_copy(
            src_ref=recv.at[tt, gg], dst_ref=recv.at[tt, gg], send_sem=fsnd.at[chip], recv_sem=frcv.at[chip],
            device_id=sibling, device_id_type=MESH)

    def from_sibling(chip):
        tt, gg = lax.div(chip, X), lax.rem(chip, X) * CORES + (1 - core)
        return pltpu.make_async_remote_copy(
            src_ref=recv.at[tt, gg], dst_ref=recv.at[tt, gg], send_sem=fsnd.at[chip], recv_sem=frcv.at[chip],
            device_id=sibling, device_id_type=MESH)

    def dscatter(xx):
        return pltpu.make_async_remote_copy(
            src_ref=dwin.at[xx], dst_ref=drecv.at[g], send_sem=dsnd.at[xx], recv_sem=drcv.at[x],
            device_id={"tm": t, "grid": xx * CORES + core}, device_id_type=MESH)

    def darrival(xx):
        return pltpu.make_async_remote_copy(
            src_ref=dwin.at[xx], dst_ref=drecv.at[xx * CORES + core], send_sem=dsnd.at[xx], recv_sem=drcv.at[xx],
            device_id={"tm": t, "grid": xx * CORES + core}, device_id_type=MESH)

    def dforward(xx):
        gg = xx * CORES + core
        return pltpu.make_async_remote_copy(
            src_ref=drecv.at[gg], dst_ref=drecv.at[gg], send_sem=dfsnd.at[xx], recv_sem=dfrcv.at[xx],
            device_id=sibling, device_id_type=MESH)

    def dfrom_sibling(xx):
        gg = xx * CORES + (1 - core)
        return pltpu.make_async_remote_copy(
            src_ref=drecv.at[gg], dst_ref=drecv.at[gg], send_sem=dfsnd.at[xx], recv_sem=dfrcv.at[xx],
            device_id=sibling, device_id_type=MESH)

    def send(j, carry):
        scatter(lax.rem(c + j, NC)).start()
        return carry

    lax.fori_loop(1, NC, send, 0)
    for j in range(1, X):
        dscatter(lax.rem(x + j, X)).start()
    cost_copy = pltpu.make_async_remote_copy(
        src_ref=misv, dst_ref=misr, send_sem=msem.at[0], recv_sem=msem.at[1],
        device_id=sibling, device_id_type=MESH)
    cost_copy.start()
    recv[t, g] = win[c]
    drecv[g] = dwin[x]
    forward(c).start()
    dforward(x).start()

    for j in range(1, X):
        xx = lax.rem(x - j + X, X)
        darrival(xx).wait_recv()
        dforward(xx).start()

    def pass_on(j, carry):
        chip = lax.rem(c - j + NC, NC)
        arrival(chip).wait_recv()
        forward(chip).start()
        return carry

    lax.fori_loop(1, NC, pass_on, 0)

    def take(chip, carry):
        from_sibling(chip).wait_recv()
        return carry

    lax.fori_loop(0, NC, take, 0)
    for xx in range(X):
        dfrom_sibling(xx).wait_recv()
    cost_copy.wait_recv()

    row = lax.broadcasted_iota(jnp.int32, (rows, LANES), 0)

    def decay(f):
        return drecv[:, f].reshape(rows, LANES)

    def forcing(tt, s, f):
        return recv[tt, :, s * NF + f].reshape(rows, LANES)

    def folded(values):
        out = None
        for v in values:
            square = v * v
            for b in range(G):
                part = square[b * TILE_ROWS : (b + 1) * TILE_ROWS]
                out = part if out is None else out + part
        return out

    zero = jnp.zeros((rows, LANES), f32)
    for f in range(NF):
        state[K, f] = zero

    def first_chain(i, carry):
        tt = T - 1 - i
        for s in reversed(range(SD)):
            k = tt * SD + s
            for f in range(NF):
                state[k, f] = decay(f) * state[k + 1, f] + forcing(tt, s, f)
        return carry

    lax.fori_loop(0, T, first_chain, 0)

    def body(i, carry):
        change, size = carry
        tt = T - 1 - i
        old = [hold[f] for f in range(NF)]
        e = [delta[f] for f in range(NF)]
        for s in reversed(range(SD)):
            k = tt * SD + s
            moved = fine(*old, row)
            here = [state[k, f] for f in range(NF)]
            new = [moved[f] + decay(f) * e[f] + forcing(tt, s, f) for f in range(NF)]
            e = [new[f] - here[f] for f in range(NF)]
            for f in range(NF):
                state[k, f] = new[f]
            emph = 1.0 + 2.0 * k.astype(f32) / (K - 1)
            change = change + emph * folded(e)
            size = size + emph * folded(new)
            old = here
        for f in range(NF):
            hold[f] = old[f]
            delta[f] = e[f]
        return change, size

    inside = (lane >= PAD) & (lane < PAD + S)
    flat = lax.broadcasted_iota(jnp.int32, (1, LANES), 1)
    sums = jnp.where(flat == 2 * ITERS, 0.5 * jnp.sum(misv[...] + misr[...]), 0.0)
    nothing = jnp.zeros((TILE_ROWS, LANES), f32)
    tail = nothing
    for n in range(ITERS):
        first = 1 if n + 1 >= SD and n > 0 else 0
        for f in range(NF):
            hold[f] = state[(T - first) * SD, f]
            delta[f] = zero
        if n == 0:
            change, tail = body(jnp.int32(0), (nothing, nothing))
            carry = lax.fori_loop(1, T, body, (change, tail))
        else:
            carry = lax.fori_loop(first, T, body, (nothing, tail if first else nothing))
        for at, value in ((n, carry[0]), (ITERS + n, carry[1])):
            sums = sums + jnp.where(flat == at, jnp.sum(jnp.where(inside, value, 0.0)), 0.0)
    srow[...] = sums

    place = lax.div(lane, S)
    q0 = lax.rem(c, R)

    def fill(chip, carry):
        tt, gg = slot(chip)
        for v in range(NV):
            packed = None
            for i in range(v * R, min((v + 1) * R, NI)):
                where = lax.rem(q0 + i, R)
                at = pl.multiple_of(gg * TILE_ROWS, TILE_ROWS)
                value = state[tt * SD + i // NF, i % NF, pl.ds(at, TILE_ROWS), :]
                turned = pltpu.roll(value, lax.rem(where * S - PAD + LANES, LANES), 1)
                packed = turned if packed is None else jnp.where(place == where, turned, packed)
            pack[chip, v] = packed
        return carry

    lax.fori_loop(0, NC, fill, 0)

    def give(chip):
        return pltpu.make_async_remote_copy(
            src_ref=pack.at[chip], dst_ref=ret.at[c], send_sem=rsnd.at[chip], recv_sem=rrcv.at[c],
            device_id=peer(chip), device_id_type=MESH)

    def got(chip):
        return pltpu.make_async_remote_copy(
            src_ref=pack.at[chip], dst_ref=ret.at[chip], send_sem=rsnd.at[chip], recv_sem=rrcv.at[chip],
            device_id=peer(chip), device_id_type=MESH)

    def tell(chip):
        return pltpu.make_async_remote_copy(
            src_ref=srow, dst_ref=sret.at[c], send_sem=ssnd.at[chip], recv_sem=srcv.at[c],
            device_id=peer(chip), device_id_type=MESH)

    def told(chip):
        return pltpu.make_async_remote_copy(
            src_ref=srow, dst_ref=sret.at[chip], send_sem=ssnd.at[chip], recv_sem=srcv.at[chip],
            device_id=peer(chip), device_id_type=MESH)

    def send_back(j, carry):
        chip = lax.rem(c + j, NC)
        tell(chip).start()
        give(chip).start()
        return carry

    lax.fori_loop(1, NC, send_back, 0)
    ret[c] = pack[c]
    sret[c] = srow[...]

    def sent(j, carry):
        chip = lax.rem(c + j, NC)
        scatter(chip).wait_send()
        forward(chip).wait_send()
        return carry

    lax.fori_loop(1, NC, sent, 0)
    forward(c).wait_send()
    for j in range(1, X):
        xx = lax.rem(x + j, X)
        dscatter(xx).wait_send()
        dforward(xx).wait_send()
    dforward(x).wait_send()
    cost_copy.wait_send()

    def receive(j, carry):
        chip = lax.rem(c - j + NC, NC)
        told(chip).wait_recv()
        got(chip).wait_recv()
        return carry

    lax.fori_loop(1, NC, receive, 0)

    for m in range(NB):
        for i in range(NI):
            value = ret[m * R, i // R]
            for q in range(1, R):
                value = jnp.where(place == (q + i) % R, ret[m * R + q, i // R], value)
            shift = (LANES - (i % R) * S) % LANES
            if shift:
                value = pltpu.roll(value, shift, 1)
            adj[i // NF, i % NF, :, m * LANES : (m + 1) * LANES] = value

    totals = sret[0]
    for m in range(1, NC):
        totals = totals + sret[m]
    ratio = totals / (pltpu.roll(totals, LANES - ITERS, 1) + epsilon)
    for n in range(ITERS):
        chg[n] = jnp.sum(jnp.where(flat == n, ratio, 0.0))
    mis[0] = jnp.sum(jnp.where(flat == 2 * ITERS, totals, 0.0))

    def done(j, carry):
        chip = lax.rem(c + j, NC)
        tell(chip).wait_send()
        give(chip).wait_send()
        return carry

    lax.fori_loop(1, NC, done, 0)


def solution(mesh, interpret=False):
    T, G = mesh.shape["tm"], mesh.shape["grid"]

    def per_device(departure, obs_weight, obs_block, coarse_decay):
        SD, OD, NF, TILE = departure.shape
        RD, NLON = coarse_decay.shape[1:]
        X = G // CORES
        NC = T * X
        S = NLON // NC
        R = LANES // S
        NI = SD * NF
        NV = -(-NI // R)
        K = T * SD
        NB = NLON // LANES
        assert RD == TILE_ROWS and TILE == TILE_ROWS * LANES and NB == TILE_ROWS
        assert S * R == LANES and S + 2 * PAD <= LANES and PAD >= 2 * STEPS * ITERS
        rows = G * TILE_ROWS
        vm = functools.partial(pltpu.VMEM, dtype=f32)
        tile = (TILE_ROWS, LANES)
        dma = pltpu.SemaphoreType.DMA
        adjoint, changes, misfit = pl.pallas_call(
            functools.partial(kernel, T, G),
            out_shape=(
                jax.ShapeDtypeStruct((SD, NF, RD, NLON), f32),
                jax.ShapeDtypeStruct((ITERS,), f32),
                jax.ShapeDtypeStruct((1,), f32),
            ),
            in_specs=[
                pl.BlockSpec(memory_space=pltpu.VMEM),
                pl.BlockSpec(memory_space=pltpu.SMEM),
                pl.BlockSpec(memory_space=pltpu.SMEM),
                pl.BlockSpec(memory_space=pltpu.VMEM),
            ],
            out_specs=(
                pl.BlockSpec(memory_space=pltpu.VMEM),
                pl.BlockSpec(memory_space=pltpu.SMEM),
                pl.BlockSpec(memory_space=pltpu.SMEM),
            ),
            scratch_shapes=[
                vm((NI * NB * TILE_ROWS, LANES)),
                vm((NC, NI) + tile),
                vm((T, G, NI) + tile),
                vm((X, NF) + tile),
                vm((G, NF) + tile),
                vm((K + 1, NF, rows, LANES)),
                vm((NF, rows, LANES)),
                vm((NF, rows, LANES)),
                vm((NC, NV) + tile),
                vm((NC, NV) + tile),
                vm((1, LANES)),
                vm((NC, 1, LANES)),
                vm((1, LANES)),
                vm((1, LANES)),
                dma((NC,)), dma((NC,)), dma((NC,)), dma((NC,)),
                dma((X,)), dma((X,)), dma((X,)), dma((X,)),
                dma((NC,)), dma((NC,)), dma((NC,)), dma((NC,)), dma((2,)),
            ],
            compiler_params=pltpu.CompilerParams(
                collective_id=0, has_side_effects=True, vmem_limit_bytes=60 * 1024 * 1024
            ),
        )(departure, obs_weight, obs_block, coarse_decay)
        return adjoint, misfit.reshape(()), changes

    return jax.shard_map(
        per_device,
        mesh=mesh,
        in_specs=(
            P("tm", "grid", None, None),
            P("tm", "grid"),
            P("tm", "grid"),
            P(None, "grid", None),
        ),
        out_specs=(P("tm", None, "grid", None), P(), P()),
        check_vma=False,
    )
```

time: 277 us -> 48.4 us (0.17)
  blocking collectives: 202 us -> 0 us
  Pallas kernels: 0 us -> 41.5 us
  waiting for transfers between devices: 31.3 us -> 0 us
  starting transfers between devices: 11.8 us -> 0 us
  other arithmetic: 11.7 us -> 0 us
  local copies, waits for them, and re-layouts: 10.8 us -> 4.29 us
  between operations: 6.44 us -> 2.32 us
    all_gather x5 -> x0, blocking collectives: 163 us -> none  [carried_in(): everything = jax.tree.map(lambda part: lax.all_gather(part, axis), value)]
    pallas_call x0 -> x1, Pallas kernels: none -> 41.5 us  [per_device(): pl.pallas_call(functools.partial(kernel, T, G), out_shape=(jax.ShapeDtype...]
    psum x1 -> x0, blocking collectives: 39 us -> none  [per_device(): misfit = lax.psum(local_misfit, ('tm', 'grid'))]
    ppermute x9 -> x0, waiting for transfers between devices: 31.3 us -> none  [the longest x3 15.7 us: padded_2(): after = lax.ppermute(first, axis, down)]
    ppermute x9 -> x0, starting transfers between devices: 11.8 us -> none  [the longest x3 4.06 us: padded_2(): after = lax.ppermute(first, axis, down)]
    slice x98 -> x0, local copies, waits for them, and re-layouts: 8.56 us -> none  [the longest x48 4.33 us: laplace(): jnp.roll(values, 1, -1)]
    another operation x29 -> x0, other arithmetic: 4.76 us -> none  [the longest x24 4.06 us: sweep_once(): return jnp.stack([height_new, zonal_new, merid_new], axis=1)]
    reduce_sum x3 -> x0, other arithmetic: 3.28 us -> none  [the longest x1 1.45 us: per_device(): local_size = jnp.sum(weights * renewed ** 2)]
  transfers between devices with their start and end apart: 9 -> 0, of which waited for: 6 -> 0; matrix products, arithmetic and copies ran while one was open for 0% -> 0% of each run, Pallas kernels for 0% -> 0%
where the time goes in v1:
time: 48.4 us; the launch traced here: 48.1 us
  Pallas kernels  41.5 us (86%)
  local copies, waits for them, and re-layouts  4.29 us (9%)
  between operations  2.32 us (5%)
    pallas_call x1, Pallas kernels, per_device(): pl.pallas_call(functools.partial(kernel, T, G), out_shape=(jax.ShapeDtype...  41.5 us
    unnamed x5, local copies, waits for them, and re-layouts  4.29 us

profile of v1, /device:TPU:0, one launch (start us, length us, event | category | flops | bytes accessed | tf_op | source)
XLA Modules:
  0.0 48.1 jit_solution(16289382480421444522)
XLA Ops:
  0.6 2.0 %copy.7.dep = f32[2,16,3,1024]{3,2,1,0:T(4,128)} copy(f32[2,16,3,1024]{3,1,2,0:T(8,128)} %param.4) | data formatting | bytes 786432 | tf_op args[0]
  2.7 41.5 %shard_map.67 = (f32[2,3,8,1024]{3,2,1,0:T(8,128)}, f32[3]{0:T(128)}, f32[1]{0:T(128)}) custom-call(f32[2,16,3,1024]{3,2,1,0:T(4,128)} %copy.7.dep, f32[2,16]{1,0:T(2,128)} %wt.1, s32[2,16]{1,0:T(2,128)} %blk.1, f32[3,8,1024]{2,1,0:T(8,128)} %dec.1), custom_call_target="tpu_custom_call" | custom-call | tf_op jit(solution)/shard_map/pallas_call | solution.py:414
  44.2 1.6 %copy.11 = f32[2,3,8,1024]{3,2,1,0:T(8,128)} copy(f32[2,3,8,1024]{3,2,1,0:T(8,128)} %get-tuple-element.12) | data formatting | bytes 393216
  45.8 0.0 copy-start
  46.4 0.1 copy-done
  46.5 0.5 %copy.13 = f32[3]{0:T(128)} copy(f32[3]{0:T(128)S(1)} %copy-done) | data formatting | bytes 24
Async XLA Ops:
  45.8 0.7 %copy-start = (f32[3]{0:T(128)S(1)}, f32[3]{0:T(128)}, u32[]{:S(2)}) copy-start(f32[3]{0:T(128)} %get-tuple-element.14) | copy-start | bytes 40

commit v2 on v1

--- a/solution.py
+++ b/solution.py
@@ -54,9 +54,9 @@
 
 
 def kernel(T, G, dep, wt, blk, dec, adj, chg, mis, *scratch):
-    (forc, win, recv, dwin, drecv, state, hold, delta, pack, ret, srow, sret, misv, misr) = scratch[:14]
+    (forc, win, recv, dwin, drecv, state, hold, sums, pack, ret, srow, sret, misv, misr) = scratch[:14]
     (snd, rcv, fsnd, frcv, dsnd, drcv, dfsnd, dfrcv, rsnd, rrcv, ssnd, srcv, msem) = scratch[14:]
-    SD, OD, NF, TILE = dep.shape
+    SD, NF, OD, TILE = dep.shape
     NLON = dec.shape[2]
     NB = NLON // LANES
     X = G // CORES
@@ -91,27 +91,30 @@
 
     sub = lax.broadcasted_iota(jnp.int32, (TILE_ROWS, LANES), 0)
     lane = lax.broadcasted_iota(jnp.int32, (TILE_ROWS, LANES), 1)
-    cost = jnp.zeros((NF, NLON), f32)
+    which = lax.broadcasted_iota(jnp.int32, (OD, LANES), 0)
+    cost = jnp.zeros((OD, LANES), f32)
     for s in range(SD):
         emph = 1.0 + 2.0 * (t * SD + s).astype(f32) / (K - 1)
         tiles = [[jnp.zeros((TILE_ROWS, LANES), f32) for _ in range(NB)] for _ in range(NF)]
+        weights = jnp.zeros((OD, LANES), f32)
         for o in range(OD):
             weight = emph * wt[s, o]
+            weights = jnp.where(which == o, weight, weights)
             choose = jnp.where(sub == blk[s, o], weight, 0.0)
-            block = dep[s, o]
-            cost = cost + (weight * block) * block
             for f in range(NF):
                 for r in range(NB):
-                    piece = dep[s, o, pl.ds(f, 1), pl.ds(r * LANES, LANES)]
+                    piece = dep[s, f, pl.ds(o, 1), pl.ds(r * LANES, LANES)]
                     tiles[f][r] = tiles[f][r] + choose * piece
+        squares = jnp.zeros((OD, LANES), f32)
+        for f in range(NF):
+            for r in range(NB):
+                piece = dep[s, f, :, pl.ds(r * LANES, LANES)]
+                squares = squares + piece * piece
+        cost = cost + weights * squares
         for f in range(NF):
             for r in range(NB):
                 forc[pl.ds((s * NF + f) * NB * TILE_ROWS + r, NB, TILE_ROWS), :] = tiles[f][r]
-    cost_row = jnp.sum(cost, axis=0, keepdims=True)
-    total = cost_row[:, :LANES]
-    for r in range(1, NB):
-        total = total + cost_row[:, r * LANES : (r + 1) * LANES]
-    misv[...] = total
+    misv[...] = jnp.sum(cost, axis=0, keepdims=True)
 
     def window(read, chip):
         start = lax.rem(chip * S - PAD + NLON, NLON)
@@ -204,22 +207,18 @@
         darrival(xx).wait_recv()
         dforward(xx).start()
 
-    def pass_on(j, carry):
-        chip = lax.rem(c - j + NC, NC)
-        arrival(chip).wait_recv()
-        forward(chip).start()
-        return carry
-
-    lax.fori_loop(1, NC, pass_on, 0)
-
-    def take(chip, carry):
-        from_sibling(chip).wait_recv()
-        return carry
-
-    lax.fori_loop(0, NC, take, 0)
-    for xx in range(X):
-        dfrom_sibling(xx).wait_recv()
-    cost_copy.wait_recv()
+    def relay(tt):
+        for xx in range(X):
+            chip = tt * X + xx
+
+            @pl.when(chip != c)
+            def _(chip=chip):
+                arrival(chip).wait_recv()
+                forward(chip).start()
+
+    def take(tt):
+        for xx in range(X):
+            from_sibling(tt * X + xx).wait_recv()
 
     row = lax.broadcasted_iota(jnp.int32, (rows, LANES), 0)
 
@@ -238,106 +237,113 @@
                 out = part if out is None else out + part
         return out
 
-    zero = jnp.zeros((rows, LANES), f32)
-    for f in range(NF):
-        state[K, f] = zero
-
-    def first_chain(i, carry):
-        tt = T - 1 - i
-        for s in reversed(range(SD)):
-            k = tt * SD + s
+    def give(chip):
+        return pltpu.make_async_remote_copy(
+            src_ref=pack.at[chip], dst_ref=ret.at[c], send_sem=rsnd.at[chip], recv_sem=rrcv.at[c],
+            device_id=peer(chip), device_id_type=MESH)
+
+    def got(chip):
+        return pltpu.make_async_remote_copy(
+            src_ref=pack.at[chip], dst_ref=ret.at[chip], send_sem=rsnd.at[chip], recv_sem=rrcv.at[chip],
+            device_id=peer(chip), device_id_type=MESH)
+
+    def tell(chip):
+        return pltpu.make_async_remote_copy(
+            src_ref=srow, dst_ref=sret.at[c], send_sem=ssnd.at[chip], recv_sem=srcv.at[c],
+            device_id=peer(chip), device_id_type=MESH)
+
+    def told(chip):
+        return pltpu.make_async_remote_copy(
+            src_ref=srow, dst_ref=sret.at[chip], send_sem=ssnd.at[chip], recv_sem=srcv.at[chip],
+            device_id=peer(chip), device_id_type=MESH)
+
+    place = lax.div(lane, S)
+    q0 = lax.rem(c, R)
+
+    def send_back(tt):
+        for xx in range(X):
+            chip = tt * X + xx
+            at = pl.multiple_of((xx * CORES + core) * TILE_ROWS, TILE_ROWS)
+            for v in range(NV):
+                packed = None
+                for i in range(v * R, min((v + 1) * R, NI)):
+                    where = lax.rem(q0 + i, R)
+                    value = hold[i // NF, i % NF, pl.ds(at, TILE_ROWS), :]
+                    turned = pltpu.roll(value, lax.rem(where * S - PAD + LANES, LANES), 1)
+                    packed = turned if packed is None else jnp.where(place == where, turned, packed)
+                pack[chip, v] = packed
+
+            @pl.when(chip != c)
+            def _(chip=chip):
+                give(chip).start()
+
+    def account(k, s, new):
+        emph = 1.0 + 2.0 * k.astype(f32) / (K - 1)
+        for n in range(ITERS):
+            if k is not last:
+                sums[n] = sums[n] + emph * folded([new[n + 1][f] - new[n][f] for f in range(NF)])
+            sums[ITERS + n] = sums[ITERS + n] + emph * folded(new[n + 1])
+        for n in range(ITERS + 1):
             for f in range(NF):
-                state[k, f] = decay(f) * state[k + 1, f] + forcing(tt, s, f)
-        return carry
-
-    lax.fori_loop(0, T, first_chain, 0)
-
-    def body(i, carry):
-        change, size = carry
-        tt = T - 1 - i
-        old = [hold[f] for f in range(NF)]
-        e = [delta[f] for f in range(NF)]
-        for s in reversed(range(SD)):
-            k = tt * SD + s
-            moved = fine(*old, row)
-            here = [state[k, f] for f in range(NF)]
-            new = [moved[f] + decay(f) * e[f] + forcing(tt, s, f) for f in range(NF)]
-            e = [new[f] - here[f] for f in range(NF)]
-            for f in range(NF):
-                state[k, f] = new[f]
-            emph = 1.0 + 2.0 * k.astype(f32) / (K - 1)
-            change = change + emph * folded(e)
-            size = size + emph * folded(new)
-            old = here
+                state[n, f] = new[n][f]
         for f in range(NF):
-            hold[f] = old[f]
-            delta[f] = e[f]
-        return change, size
+            hold[s, f] = new[ITERS][f]
+
+    last = jnp.int32(K - 1)
+    relay(T - 1)
+    if T > 1:
+        relay(T - 2)
+    take(T - 1)
+    sums[...] = jnp.zeros(sums.shape, f32)
+    account(last, SD - 1, [[forcing(T - 1, SD - 1, f) for f in range(NF)]] * (ITERS + 1))
+    for xx in range(X):
+        dfrom_sibling(xx).wait_recv()
+
+    if SD == 1:
+        send_back(T - 1)
+
+    def step(i, carry):
+        k = K - 2 - i
+        tt = lax.div(k, SD)
+        s = lax.rem(k, SD)
+
+        @pl.when(s == SD - 1)
+        def _():
+            @pl.when(tt > 0)
+            def _():
+                relay(tt - 1)
+            take(tt)
+
+        old = [[state[n, f] for f in range(NF)] for n in range(ITERS + 1)]
+        force = [recv[tt, :, s * NF + f].reshape(rows, LANES) for f in range(NF)]
+        d = [decay(f) for f in range(NF)]
+        new = [[d[f] * old[0][f] + force[f] for f in range(NF)]]
+        for n in range(ITERS):
+            moved = fine(*old[n], row)
+            new.append([moved[f] + d[f] * (old[n + 1][f] - old[n][f]) + force[f] for f in range(NF)])
+        account(k, s, new)
+
+        @pl.when(s == 0)
+        def _():
+            send_back(tt)
+
+        return carry
+
+    lax.fori_loop(0, K - 1, step, 0)
 
     inside = (lane >= PAD) & (lane < PAD + S)
     flat = lax.broadcasted_iota(jnp.int32, (1, LANES), 1)
-    sums = jnp.where(flat == 2 * ITERS, 0.5 * jnp.sum(misv[...] + misr[...]), 0.0)
-    nothing = jnp.zeros((TILE_ROWS, LANES), f32)
-    tail = nothing
-    for n in range(ITERS):
-        first = 1 if n + 1 >= SD and n > 0 else 0
-        for f in range(NF):
-            hold[f] = state[(T - first) * SD, f]
-            delta[f] = zero
-        if n == 0:
-            change, tail = body(jnp.int32(0), (nothing, nothing))
-            carry = lax.fori_loop(1, T, body, (change, tail))
-        else:
-            carry = lax.fori_loop(first, T, body, (nothing, tail if first else nothing))
-        for at, value in ((n, carry[0]), (ITERS + n, carry[1])):
-            sums = sums + jnp.where(flat == at, jnp.sum(jnp.where(inside, value, 0.0)), 0.0)
-    srow[...] = sums
-
-    place = lax.div(lane, S)
-    q0 = lax.rem(c, R)
-
-    def fill(chip, carry):
-        tt, gg = slot(chip)
-        for v in range(NV):
-            packed = None
-            for i in range(v * R, min((v + 1) * R, NI)):
-                where = lax.rem(q0 + i, R)
-                at = pl.multiple_of(gg * TILE_ROWS, TILE_ROWS)
-                value = state[tt * SD + i // NF, i % NF, pl.ds(at, TILE_ROWS), :]
-                turned = pltpu.roll(value, lax.rem(where * S - PAD + LANES, LANES), 1)
-                packed = turned if packed is None else jnp.where(place == where, turned, packed)
-            pack[chip, v] = packed
-        return carry
-
-    lax.fori_loop(0, NC, fill, 0)
-
-    def give(chip):
-        return pltpu.make_async_remote_copy(
-            src_ref=pack.at[chip], dst_ref=ret.at[c], send_sem=rsnd.at[chip], recv_sem=rrcv.at[c],
-            device_id=peer(chip), device_id_type=MESH)
-
-    def got(chip):
-        return pltpu.make_async_remote_copy(
-            src_ref=pack.at[chip], dst_ref=ret.at[chip], send_sem=rsnd.at[chip], recv_sem=rrcv.at[chip],
-            device_id=peer(chip), device_id_type=MESH)
-
-    def tell(chip):
-        return pltpu.make_async_remote_copy(
-            src_ref=srow, dst_ref=sret.at[c], send_sem=ssnd.at[chip], recv_sem=srcv.at[c],
-            device_id=peer(chip), device_id_type=MESH)
-
-    def told(chip):
-        return pltpu.make_async_remote_copy(
-            src_ref=srow, dst_ref=sret.at[chip], send_sem=ssnd.at[chip], recv_sem=srcv.at[chip],
-            device_id=peer(chip), device_id_type=MESH)
-
-    def send_back(j, carry):
-        chip = lax.rem(c + j, NC)
-        tell(chip).start()
-        give(chip).start()
-        return carry
-
-    lax.fori_loop(1, NC, send_back, 0)
+    cost_copy.wait_recv()
+    line = jnp.where(flat == 2 * ITERS, 0.5 * jnp.sum(misv[...] + misr[...]), 0.0)
+    for n in range(2 * ITERS):
+        line = line + jnp.where(flat == n, jnp.sum(jnp.where(inside, sums[n], 0.0)), 0.0)
+    srow[...] = line
+
+    def tell_all(j, carry):
+        tell(lax.rem(c + j, NC)).start()
+        return carry
+
+    lax.fori_loop(1, NC, tell_all, 0)
     ret[c] = pack[c]
     sret[c] = srow[...]
 
@@ -435,9 +441,9 @@
                 vm((T, G, NI) + tile),
                 vm((X, NF) + tile),
                 vm((G, NF) + tile),
-                vm((K + 1, NF, rows, LANES)),
-                vm((NF, rows, LANES)),
-                vm((NF, rows, LANES)),
+                vm((ITERS + 1, NF, rows, LANES)),
+                vm((SD, NF, rows, LANES)),
+                vm((2 * ITERS,) + tile),
                 vm((NC, NV) + tile),
                 vm((NC, NV) + tile),
                 vm((1, LANES)),
@@ -451,7 +457,7 @@
             compiler_params=pltpu.CompilerParams(
                 collective_id=0, has_side_effects=True, vmem_limit_bytes=60 * 1024 * 1024
             ),
-        )(departure, obs_weight, obs_block, coarse_decay)
+        )(departure.transpose(0, 2, 1, 3), obs_weight, obs_block, coarse_decay)
         return adjoint, misfit.reshape(()), changes
 
     return jax.shard_map(

time: 48.4 us -> 38.8 us (0.80)
  Pallas kernels: 41.5 us -> 34 us
  local copies, waits for them, and re-layouts: 4.29 us -> 2.13 us
    pallas_call x1, Pallas kernels: 41.5 us -> 34 us  [per_device(): pl.pallas_call(functools.partial(kernel, T, G), out_shape=(jax.ShapeDtype...]
    unnamed x5 -> x4, local copies, waits for them, and re-layouts: 4.29 us -> 2.13 us
where the time goes in v2:
time: 38.8 us; the launch traced here: 38.6 us
  Pallas kernels  34 us (88%)
  between operations  2.41 us (6%)
  local copies, waits for them, and re-layouts  2.13 us (5%)
    pallas_call x1, Pallas kernels, per_device(): pl.pallas_call(functools.partial(kernel, T, G), out_shape=(jax.ShapeDtype...  34 us
    unnamed x4, local copies, waits for them, and re-layouts  2.13 us

profile of v2, /device:TPU:0, one launch (start us, length us, event | category | flops | bytes accessed | tf_op | source)
XLA Modules:
  0.0 38.6 jit_solution(3725620359485888563)
XLA Ops:
  0.6 34.0 %shard_map.67 = (f32[2,3,8,1024]{3,2,1,0:T(8,128)}, f32[3]{0:T(128)}, f32[1]{0:T(128)}) custom-call(f32[2,3,16,1024]{3,2,1,0:T(8,128)} %bitcast.2, f32[2,16]{1,0:T(2,128)} %wt.1, s32[2,16]{1,0:T(2,128)} %blk.1, f32[3,8,1024]{2,1,0:T(8,128)} %dec.1), custom_call_target="tpu_custom_call" | custom-call | tf_op jit(solution)/shard_map/pallas_call | solution.py:420
  34.7 1.6 %copy.10 = f32[2,3,8,1024]{3,2,1,0:T(8,128)} copy(f32[2,3,8,1024]{3,2,1,0:T(8,128)} %get-tuple-element.12) | data formatting | bytes 393216
  36.3 0.0 copy-start
  36.9 0.0 copy-done
  36.9 0.5 %copy.12 = f32[3]{0:T(128)} copy(f32[3]{0:T(128)S(1)} %copy-done) | data formatting | bytes 24
Async XLA Ops:
  36.3 0.6 %copy-start = (f32[3]{0:T(128)S(1)}, f32[3]{0:T(128)}, u32[]{:S(2)}) copy-start(f32[3]{0:T(128)} %get-tuple-element.14) | copy-start | bytes 40

commit v3 on v2

--- a/solution.py
+++ b/solution.py
@@ -23,39 +23,61 @@
 f32 = jnp.float32
 
 
-def fine(p, q, r, row):
-    rows = p.shape[0]
+def fine(p, q, r, sub):
+    count = p.shape[0] // TILE_ROWS
+
+    def blocks(v):
+        return [v[b * TILE_ROWS : (b + 1) * TILE_ROWS] for b in range(count)]
 
     def west_east(v):
-        return pltpu.roll(v, 1, 1), pltpu.roll(v, LANES - 1, 1)
+        return [pltpu.roll(b, 1, 1) for b in v], [pltpu.roll(b, LANES - 1, 1) for b in v]
 
     def up_down(v):
-        above = jnp.where(row == 0, 0.0, pltpu.roll(v, 1, 0))
-        below = jnp.where(row == rows - 1, 0.0, pltpu.roll(v, rows - 1, 0))
+        less = [jnp.zeros_like(v[0])] + [pltpu.roll(b, 1, 0) for b in v]
+        more = [pltpu.roll(b, TILE_ROWS - 1, 0) for b in v] + [jnp.zeros_like(v[0])]
+        above = [jnp.where(sub == 0, less[b], less[b + 1]) for b in range(count)]
+        below = [jnp.where(sub == TILE_ROWS - 1, more[b + 1], more[b]) for b in range(count)]
         return above, below
 
-    half = 0.5 * wave_coef
+    ratio = 0.5 * wave_coef / diffusion
     keep = 1.0 - 4.0 * diffusion
+    every = range(count)
+    p, q, r = [ratio * v for v in blocks(p)], blocks(q), blocks(r)
+    pw, pe = west_east(p)
+    pu, pd = up_down(p)
     for _ in range(STEPS):
-        pw, pe = west_east(p)
-        pu, pd = up_down(p)
         qw, qe = west_east(q)
         qu, qd = up_down(q)
         rw, re = west_east(r)
         ru, rd = up_down(r)
-        p = keep * p + half * ((qe - qw) + (rd - ru)) + diffusion * ((pw + pe) + (pu + pd))
-        nw, ne = west_east(p)
-        nu, nd = up_down(p)
+        p = [
+            keep * p[b]
+            + (0.5 * wave_coef * ratio) * ((qe[b] - qw[b]) + (rd[b] - ru[b]))
+            + diffusion * ((pw[b] + pe[b]) + (pu[b] + pd[b]))
+            for b in every
+        ]
+        pw, pe = west_east(p)
+        pu, pd = up_down(p)
+        turn = coriolis / diffusion
         q, r = (
-            keep * q + half * (ne - nw) + coriolis * r + diffusion * ((qw + qe) + (qu + qd)),
-            keep * r + half * (nd - nu) - coriolis * q + diffusion * ((rw + re) + (ru + rd)),
+            [
+                keep * q[b]
+                + diffusion * (((pe[b] - pw[b]) + turn * r[b]) + ((qw[b] + qe[b]) + (qu[b] + qd[b])))
+                for b in every
+            ],
+            [
+                keep * r[b]
+                + diffusion * (((pd[b] - pu[b]) - turn * q[b]) + ((rw[b] + re[b]) + (ru[b] + rd[b])))
+                for b in every
+            ],
         )
-    return p, q, r
-
-
-def kernel(T, G, dep, wt, blk, dec, adj, chg, mis, *scratch):
-    (forc, win, recv, dwin, drecv, state, hold, sums, pack, ret, srow, sret, misv, misr) = scratch[:14]
-    (snd, rcv, fsnd, frcv, dsnd, drcv, dfsnd, dfrcv, rsnd, rrcv, ssnd, srcv, msem) = scratch[14:]
+    p = [(1.0 / ratio) * v for v in p]
+    return [jnp.concatenate(v, axis=0) for v in (p, q, r)]
+
+
+def kernel(T, G, dep_hbm, wt, blk, dec_hbm, ret, sret, *scratch):
+    (forc, win, recv, dwin, drecv, state, hold, sums, pack, srow, misv, misr, dep, dec) = scratch[:14]
+    (snd, rcv, fsnd, frcv, dsnd, drcv, dfsnd, dfrcv, rsnd, rrcv, ssnd, srcv, msem, isem) = scratch[14:]
     SD, NF, OD, TILE = dep.shape
     NLON = dec.shape[2]
     NB = NLON // LANES
@@ -88,6 +110,12 @@
 
     lax.fori_loop(1, NC, greet, 0)
     pl.semaphore_signal(barrier, inc=1, device_id=sibling, device_id_type=MESH)
+
+    dec_copy = pltpu.make_async_copy(dec_hbm, dec, isem.at[0])
+    dep_copy = pltpu.make_async_copy(dep_hbm, dep, isem.at[1])
+    dep_copy.start()
+    dec_copy.start()
+    dep_copy.wait()
 
     sub = lax.broadcasted_iota(jnp.int32, (TILE_ROWS, LANES), 0)
     lane = lax.broadcasted_iota(jnp.int32, (TILE_ROWS, LANES), 1)
@@ -133,6 +161,7 @@
         return carry
 
     lax.fori_loop(0, NC, cut, 0)
+    dec_copy.wait()
     for xx in range(X):
         for f in range(NF):
             def read(b, f=f):
@@ -187,10 +216,14 @@
             device_id=sibling, device_id_type=MESH)
 
     def send(j, carry):
-        scatter(lax.rem(c + j, NC)).start()
-        return carry
-
-    lax.fori_loop(1, NC, send, 0)
+        chip = NC - 1 - j
+
+        @pl.when(chip != c)
+        def _():
+            scatter(chip).start()
+        return carry
+
+    lax.fori_loop(0, NC, send, 0)
     for j in range(1, X):
         dscatter(lax.rem(x + j, X)).start()
     cost_copy = pltpu.make_async_remote_copy(
@@ -220,7 +253,6 @@
         for xx in range(X):
             from_sibling(tt * X + xx).wait_recv()
 
-    row = lax.broadcasted_iota(jnp.int32, (rows, LANES), 0)
 
     def decay(f):
         return drecv[:, f].reshape(rows, LANES)
@@ -319,7 +351,7 @@
         d = [decay(f) for f in range(NF)]
         new = [[d[f] * old[0][f] + force[f] for f in range(NF)]]
         for n in range(ITERS):
-            moved = fine(*old[n], row)
+            moved = fine(*old[n], sub)
             new.append([moved[f] + d[f] * (old[n + 1][f] - old[n][f]) + force[f] for f in range(NF)])
         account(k, s, new)
 
@@ -370,6 +402,23 @@
 
     lax.fori_loop(1, NC, receive, 0)
 
+    def done(j, carry):
+        chip = lax.rem(c + j, NC)
+        tell(chip).wait_send()
+        give(chip).wait_send()
+        return carry
+
+    lax.fori_loop(1, NC, done, 0)
+
+
+def finish(S, ret, sret, adj, chg, mis):
+    SD, NF, RD, NLON = adj.shape
+    NC = ret.shape[0]
+    NI = SD * NF
+    NB = NLON // LANES
+    R = LANES // S
+    place = lax.div(lax.broadcasted_iota(jnp.int32, (TILE_ROWS, LANES), 1), S)
+    flat = lax.broadcasted_iota(jnp.int32, (1, LANES), 1)
     for m in range(NB):
         for i in range(NI):
             value = ret[m * R, i // R]
@@ -387,14 +436,6 @@
     for n in range(ITERS):
         chg[n] = jnp.sum(jnp.where(flat == n, ratio, 0.0))
     mis[0] = jnp.sum(jnp.where(flat == 2 * ITERS, totals, 0.0))
-
-    def done(j, carry):
-        chip = lax.rem(c + j, NC)
-        tell(chip).wait_send()
-        give(chip).wait_send()
-        return carry
-
-    lax.fori_loop(1, NC, done, 0)
 
 
 def solution(mesh, interpret=False):
@@ -417,23 +458,21 @@
         vm = functools.partial(pltpu.VMEM, dtype=f32)
         tile = (TILE_ROWS, LANES)
         dma = pltpu.SemaphoreType.DMA
-        adjoint, changes, misfit = pl.pallas_call(
+        back, lines = pl.pallas_call(
             functools.partial(kernel, T, G),
             out_shape=(
-                jax.ShapeDtypeStruct((SD, NF, RD, NLON), f32),
-                jax.ShapeDtypeStruct((ITERS,), f32),
-                jax.ShapeDtypeStruct((1,), f32),
+                jax.ShapeDtypeStruct((NC, NV) + tile, f32),
+                jax.ShapeDtypeStruct((NC, 1, LANES), f32),
             ),
             in_specs=[
-                pl.BlockSpec(memory_space=pltpu.VMEM),
+                pl.BlockSpec(memory_space=pltpu.HBM),
                 pl.BlockSpec(memory_space=pltpu.SMEM),
                 pl.BlockSpec(memory_space=pltpu.SMEM),
-                pl.BlockSpec(memory_space=pltpu.VMEM),
+                pl.BlockSpec(memory_space=pltpu.HBM),
             ],
             out_specs=(
                 pl.BlockSpec(memory_space=pltpu.VMEM),
-                pl.BlockSpec(memory_space=pltpu.SMEM),
-                pl.BlockSpec(memory_space=pltpu.SMEM),
+                pl.BlockSpec(memory_space=pltpu.VMEM),
             ),
             scratch_shapes=[
                 vm((NI * NB * TILE_ROWS, LANES)),
@@ -445,19 +484,34 @@
                 vm((SD, NF, rows, LANES)),
                 vm((2 * ITERS,) + tile),
                 vm((NC, NV) + tile),
-                vm((NC, NV) + tile),
-                vm((1, LANES)),
-                vm((NC, 1, LANES)),
                 vm((1, LANES)),
                 vm((1, LANES)),
+                vm((1, LANES)),
+                vm((SD, NF, OD, NLON)),
+                vm((NF, RD, NLON)),
                 dma((NC,)), dma((NC,)), dma((NC,)), dma((NC,)),
                 dma((X,)), dma((X,)), dma((X,)), dma((X,)),
-                dma((NC,)), dma((NC,)), dma((NC,)), dma((NC,)), dma((2,)),
+                dma((NC,)), dma((NC,)), dma((NC,)), dma((NC,)), dma((2,)), dma((2,)),
             ],
             compiler_params=pltpu.CompilerParams(
                 collective_id=0, has_side_effects=True, vmem_limit_bytes=60 * 1024 * 1024
             ),
         )(departure.transpose(0, 2, 1, 3), obs_weight, obs_block, coarse_decay)
+        adjoint, changes, misfit = pl.pallas_call(
+            functools.partial(finish, S),
+            out_shape=(
+                jax.ShapeDtypeStruct((SD, NF, RD, NLON), f32),
+                jax.ShapeDtypeStruct((ITERS,), f32),
+                jax.ShapeDtypeStruct((1,), f32),
+            ),
+            in_specs=[pl.BlockSpec(memory_space=pltpu.VMEM)] * 2,
+            out_specs=(
+                pl.BlockSpec(memory_space=pltpu.VMEM),
+                pl.BlockSpec(memory_space=pltpu.SMEM),
+                pl.BlockSpec(memory_space=pltpu.SMEM),
+            ),
+            compiler_params=pltpu.CompilerParams(vmem_limit_bytes=60 * 1024 * 1024),
+        )(back, lines)
         return adjoint, misfit.reshape(()), changes
 
     return jax.shard_map(

time: 38.8 us -> 36.3 us (0.936)
  local copies, waits for them, and re-layouts: 2.13 us -> 0 us
  between operations: 2.41 us -> 0.64 us
  Pallas kernels: 34 us -> 35.5 us
    unnamed x4 -> x0, local copies, waits for them, and re-layouts: 2.13 us -> none
    pallas_call x0 -> x1, Pallas kernels: none -> 1.81 us  [per_device(): pl.pallas_call(functools.partial(finish, S), out_shape=(jax.ShapeDtypeStr...]
where the time goes in v3:
time: 36.3 us; the launch traced here: 36.1 us
  Pallas kernels  35.5 us (98%)
  between operations  0.64 us (2%)
    pallas_call x1, Pallas kernels, per_device(): pl.pallas_call(functools.partial(kernel, T, G), out_shape=(jax.ShapeDtype...  33.7 us
    pallas_call x1, Pallas kernels, per_device(): pl.pallas_call(functools.partial(finish, S), out_shape=(jax.ShapeDtypeStr...  1.81 us

profile of v3, /device:TPU:0, one launch (start us, length us, event | category | flops | bytes accessed | tf_op | source)
XLA Modules:
  0.0 36.1 jit_solution(2023859925407839640)
XLA Ops:
  0.6 33.7 %shard_map.67 = (f32[16,3,8,128]{3,2,1,0:T(8,128)}, f32[16,1,128]{2,1,0:T(1,128)}) custom-call(f32[2,3,16,1024]{3,2,1,0:T(8,128)} %bitcast.2, f32[2,16]{1,0:T(2,128)} %wt.1, s32[2,16]{1,0:T(2,128)} %blk.1, f32[3,8,1024]{2,1,0:T(8,128)} %dec_hbm.1), custom_call_target="tpu_custom_call" | custom-call | tf_op jit(solution)/shard_map/pallas_call | solution.py:461
  34.3 1.8 %shard_map.68 = (f32[2,3,8,1024]{3,2,1,0:T(8,128)}, f32[3]{0:T(128)}, f32[1]{0:T(128)}) custom-call(f32[16,3,8,128]{3,2,1,0:T(8,128)} %get-tuple-element.8.ret, f32[16,1,128]{2,1,0:T(1,128)} %get-tuple-element.9.sret), custom_call_target="tpu_custom_call" | custom-call | tf_op jit(solution)/shard_map/pallas_call | solution.py:500
